TPU v7x, 512 devices: a whole 4x4x16 slice. The times are simulated.
512 devices in a mesh: layer: 8 (over y, core), latent: 64 (over x, z).
Axes of the slice: x: 4, y: 4, z: 16, core: 2. Of those that a mesh axis runs over, the one named last changes fastest.
Arguments:
- resid: bfloat16 [4, 128, 3584], P(None, 'latent'), may hold values from -6 to 6
- target: bfloat16 [5, 128, 3584], P(None, 'latent'), may hold values from -6 to 6
- enc_weight: bfloat16 [8, 3584, 8192], P('layer', None, 'latent'), may hold values from -0.09375 to 0.09375
- enc_bias: float32 [8, 8192], P('layer', 'latent'), may hold values from -3 to 3
- dec_weight: bfloat16 [8, 2, 2, 8192, 1792], P('layer', None, None, 'latent'), may hold values from -0.046875 to 0.046875
- blocks: int32 [4, 1, 96], replicated, may hold values from 0 to 127, all different within a row
Outputs:
- errors: bfloat16 [8, 128, 1792], P('layer', 'latent')
- enc_grad: bfloat16 [8, 3584, 8192], P('layer', None, 'latent')
- bias_grad: float32 [8, 8192], P('layer', 'latent')
Inputs may be any that keep to these rules, and one draw needn't show every extreme that they name: Each row names 96 different blocks; every block is named in some row.
All inputs are finite; a program needn't handle non-finite values.
Results may differ from a plain program's by a relative error of at most 0.007.
Values may be sent and summed in bfloat16 or wider, within the bound.
A program may use at most 64 MiB of HBM per device.

v0:
```python
import jax
import jax.numpy as jnp
from jax import lax
from jax.sharding import Mesh
from jax.sharding import PartitionSpec as P

LATENT = ("latent_0", "latent_1")


def laid_out(pieces, dim):
    pieces = jnp.moveaxis(pieces, 0, dim)
    shape = pieces.shape
    return pieces.reshape(*shape[:dim], shape[dim] * shape[dim + 1], *shape[dim + 2 :])


def all_blocks(shard, axes, sequence):
    pieces = shard[None]
    for k in sequence:
        pieces = lax.all_gather(pieces, axes[k], axis=0, tiled=True)
    held = [lax.axis_size(axes[k]) for k in reversed(sequence)]
    pieces = pieces.reshape(*held, *shard.shape)
    turned = sorted(range(len(sequence)), key=lambda place: sequence[len(sequence) - 1 - place])
    return pieces.transpose(*turned, *range(len(sequence), pieces.ndim)).reshape(-1, *shard.shape)


def gathered_by_axis(shard, axes, sequence, dim):
    return laid_out(all_blocks(shard, axes, sequence), dim)


def swapped(shard, axis, stride):
    return lax.ppermute(shard, axis, [(i, i ^ 1 << stride) for i in range(lax.axis_size(axis))])


def split_up(shard, dim, count):
    shape = shard.shape
    pieces = shard.reshape(*shape[:dim], count, shape[dim] // count, *shape[dim + 1 :])
    return jnp.moveaxis(pieces, dim, 0)


def sent_and_summed(shard, axis, dim):
    count = lax.axis_size(axis)
    pieces = lax.all_to_all(split_up(shard, dim, count), axis, 0, 0, tiled=True)
    return jnp.sum(pieces, axis=0)


def summed_rows(shard, axes, dim):
    far, near = axes
    return sent_and_summed(sent_and_summed(shard, far, dim), near, dim)


def from_behind(block, axis, distance):
    devices = range(lax.axis_size(axis))
    route = [(i - distance, i) for i in devices if i - distance in devices]
    return lax.ppermute(block, axis, route)


def sent_to_all(shard, axis):
    count = lax.axis_size(axis)
    return lax.all_to_all(
        jnp.broadcast_to(shard[None], (count, *shard.shape)), axis, 0, 0, tiled=True
    )


def gathered_copies(shard, axis, dim):
    return laid_out(sent_to_all(shard, axis), dim)


def in_one_piece(arrays, axis, dim, along):
    ends, at = ([], 0)
    for a in arrays[:-1]:
        at += a.shape[along]
        ends.append(at)
    both = jnp.concatenate(arrays, axis=along)
    return tuple(jnp.split(gathered_copies(both, axis, dim), ends, axis=along))


def contract_rows(left_rows, right_rows):
    return lax.dot_general(
        left_rows, right_rows, (((0,), (0,)), ((), ())), preferred_element_type=jnp.float32
    )


def contract_cols(left_rows, right_rows):
    return lax.dot_general(
        left_rows, right_rows, (((1,), (1,)), ((), ())), preferred_element_type=jnp.float32
    )


def on_device(resid, target, enc_weight, enc_bias, dec_weight, blocks):
    latent_devices = lax.axis_size(LATENT)
    layer_slot = lax.axis_index("layer")
    layer_row = layer_slot // 2
    which_half = layer_slot % 2
    column_pos = lax.axis_index(LATENT)
    rows_in = lax.dynamic_index_in_dim(resid, layer_row, 0, keepdims=False)
    local_rows = rows_in.shape[0]
    token_count = local_rows * latent_devices
    weight_in = enc_weight[0]
    block_width = weight_in.shape[1]
    decoder = dec_weight[0]
    column_width = decoder.shape[-1]
    dec_own = decoder[0].reshape(2 * block_width, column_width)
    dec_next = decoder[1].reshape(2 * block_width, column_width)
    listed = lax.dynamic_index_in_dim(blocks, layer_row, 0, keepdims=False)
    tile_len = token_count // listed.shape[0]
    flags = jnp.any(listed == which_half * latent_devices + column_pos, axis=1).astype(jnp.float32)
    gate_mask = jnp.repeat(flags, tile_len)[:, None]
    whole_in = gathered_by_axis(rows_in, LATENT, (0, 1), 0)
    preact = jnp.dot(whole_in, weight_in, preferred_element_type=jnp.float32)
    preact = preact + enc_bias[0][None, :]
    latents_on = (preact * gate_mask).astype(jnp.bfloat16)
    partner = swapped(latents_on, "layer", 0)
    lower_half = jnp.where(which_half == 0, latents_on, partner)
    upper_half = jnp.where(which_half == 0, partner, latents_on)
    pair_acts = jnp.concatenate([lower_half, upper_half], axis=1)
    totals = summed_rows(
        jnp.concatenate(
            [
                jnp.dot(pair_acts, dec_own, preferred_element_type=jnp.float32),
                jnp.dot(pair_acts, dec_next, preferred_element_type=jnp.float32),
            ],
            axis=1,
        ),
        ("latent_0", "latent_1"),
        0,
    )
    own_sum = totals[:, :column_width]
    ahead_part = totals[:, column_width:]
    targets = lax.dynamic_slice_in_dim(target, layer_row, 2, 0)
    targets = lax.dynamic_slice_in_dim(targets, which_half * column_width, column_width, 2).astype(
        jnp.float32
    )
    behind = from_behind(ahead_part, "layer", 2)
    err_own = (own_sum + behind - targets[0]).astype(jnp.bfloat16)
    next_own = from_behind(own_sum, "layer", -2)
    err_next = (next_own + ahead_part - targets[1]).astype(jnp.bfloat16)
    piece_pair = in_one_piece((err_own, err_next), LATENT, 0, 1)
    grad_pair = contract_cols(piece_pair[0], dec_own) + contract_cols(piece_pair[1], dec_next)
    lower_grad = grad_pair[:, :block_width]
    upper_grad = grad_pair[:, block_width:]
    own_part = jnp.where(which_half == 0, lower_grad, upper_grad)
    their_part = jnp.where(which_half == 0, upper_grad, lower_grad)
    received = swapped(their_part, "layer", 0)
    grad_pre = (own_part + received) * gate_mask
    bias_grad = jnp.sum(grad_pre, axis=0)[None, :]
    grad_low = grad_pre.astype(jnp.bfloat16)
    grad_weight = contract_rows(whole_in, grad_low)
    return (err_own[None], grad_weight.astype(jnp.bfloat16)[None], bias_grad)


def solution(mesh):
    finer = Mesh(
        mesh.devices.reshape(mesh.shape["layer"], 4, 16), ("layer", "latent_0", "latent_1")
    )
    placed = (
        P(None, LATENT, None),
        P(None, LATENT, None),
        P("layer", None, LATENT),
        P("layer", LATENT),
        P("layer", None, None, LATENT, None),
        P(),
    )
    return jax.shard_map(
        on_device,
        mesh=finer,
        in_specs=placed,
        out_specs=(P("layer", LATENT, None), P("layer", None, LATENT), P("layer", LATENT)),
        check_vma=False,
    )
```

profile of v0, /device:TPU:1, one launch (start us, length us, event | category | flops | bytes accessed | tf_op | source)
XLA Modules:
  0.0 202.1 jit_solution(11026004268313117025)
XLA Ops:
  0.6 0.0 copy-start
  0.7 0.8 constant_dynamic-slice_fusion.1
  1.5 10.2 %all_gather.6 = bf16[4,2,3584]{2,1,0:T(2,128)(2,1)S(1)} all-gather(bf16[1,2,3584]{2,1,0:T(2,128)(2,1)S(1)} %constant_dynamic-slice_fusion.1), channel_id=1, replica_groups=mesh['layer'=8,'latent_0'=4,'latent_1'=16] {'latent_0'}, dimensions={0}, use_global_device_ids=true | all-gather | bytes 71680 | tf_op jit(solution)/shard_map/all_gather | solution.py:19
  11.6 34.1 %all_gather.7 = bf16[64,2,3584]{2,1,0:T(2,128)(2,1)S(1)} all-gather(bf16[4,2,3584]{2,1,0:T(2,128)(2,1)S(1)} %all_gather.6), channel_id=1, replica_groups=mesh['layer'=8,'latent_0'=4,'latent_1'=16] {'latent_1'}, dimensions={0}, use_global_device_ids=true | all-gather | bytes 974848 | tf_op jit(solution)/shard_map/all_gather | solution.py:19
  45.7 0.0 copy-start.3
  45.7 0.6 copy.30
  46.4 0.3 reshape_reshape.3
  46.7 1.3 compare_reduce_fusion
  48.7 0.0 copy-start.1
  48.7 0.0 copy-done
  48.7 0.0 copy-done.3
  48.7 0.5 fusion.2
  49.2 12.2 %collective-permute-start = (bf16[128,128]{0,1:T(8,128)(2,1)S(1)}, bf16[128,128]{0,1:T(8,128)(2,1)S(1)}, u32[]{:S(2)}, u32[]{:S(2)}) collective-permute-start(bf16[128,128]{0,1:T(8,128)(2,1)S(1)} %fusion.2), channel_id=1, source_target_pairs={{0,64},{64,0},{128,192},{192,128},{256,320},{320,256},{384,448},{4... | collective-permute-start | bytes 98312 | tf_op jit(solution)/shard_map/ppermute | solution.py:31
  61.3 0.0 copy-done.1
  61.4 1.0 fusion.17
  62.4 0.0 collective-permute-done
  62.4 1.5 fusion.8
  63.9 0.3 fusion.7
  64.2 0.2 pad_maximum_fusion
  64.4 26.5 %all_to_all.15 = f32[4,32,3584]{2,1,0:T(8,128)} all-to-all(f32[4,32,3584]{2,1,0:T(8,128)S(1)} %bitcast.38), channel_id=1, replica_groups=mesh['layer'=8,'latent_0'=4,'latent_1'=16] {'latent_0'}, dimensions={0} | all-to-all | bytes 3670016 | tf_op jit(solution)/shard_map/all_to_all | solution.py:42
  91.0 1.6 reduce_sum.27
  92.6 1.0 reshape.43
  93.6 6.7 %all-to-all-start.1 = ((f32[16,2,3584]{2,1,0:T(2,128)}), f32[16,2,3584]{2,1,0:T(2,128)S(1)}, u32[]{:S(2)}, u32[]{:S(2)}) async-start(f32[16,2,3584]{2,1,0:T(2,128)} %reshape.43), calls=%async_computation.1 | async-start | bytes 917504 | tf_op jit(solution)/shard_map/all_to_all | solution.py:42
  100.4 20.8 %all-to-all-done.1 = f32[16,2,3584]{2,1,0:T(2,128)S(1)} async-done(((f32[16,2,3584]{2,1,0:T(2,128)}), f32[16,2,3584]{2,1,0:T(2,128)S(1)}, u32[]{:S(2)}, u32[]{:S(2)}) %all-to-all-start.1) | async-done | bytes 458784 | tf_op jit(solution)/shard_map/all_to_all | solution.py:42
  121.3 0.1 reduce_sum.28
  121.4 3.2 %collective-permute-start.1 = (f32[2,1792]{1,0:T(2,128)S(1)}, f32[2,1792]{1,0:T(2,128)S(1)}, u32[]{:S(2)}, u32[]{:S(2)}) collective-permute-start(f32[2,1792]{1,0:T(2,128)S(1)} %get-tuple-element.12), channel_id=1, source_target_pairs={{0,128},{64,192},{128,256},{192,320},{256,384},{320,448},{1,129},{... | collective-permute-start | bytes 43016 | tf_op jit(solution)/shard_map/ppermute | solution.py:54
  124.6 1.3 collective-permute-start.2
  125.9 0.8 dynamic-slice_convert_fusion
  126.7 0.0 collective-permute-done.1
  126.7 2.3 %collective-permute-done.2 = f32[2,1792]{1,0:T(2,128)S(1)} collective-permute-done((f32[2,1792]{1,0:T(2,128)S(1)}, f32[2,1792]{1,0:T(2,128)S(1)}, u32[]{:S(2)}, u32[]{:S(2)}) %collective-permute-start.2) | collective-permute-done | bytes 14368 | tf_op jit(solution)/shard_map/ppermute | solution.py:54
  129.1 0.0 copy-start.2
  129.1 0.5 broadcast_in_dim.18
  129.6 56.9 %all_to_all.16 = bf16[64,2,3584]{2,1,0:T(2,128)(2,1)} all-to-all(bf16[64,2,3584]{2,1,0:T(2,128)(2,1)S(1)} %broadcast_in_dim.18), channel_id=1, replica_groups=mesh['layer'=8,'latent_0'=4,'latent_1'=16] {'latent_0','latent_1'}, dimensions={0} | all-to-all | bytes 1835008 | tf_op jit(solution)/shard_map/all_to_all | solution.py:59
  186.5 3.2 %reshape.44 = bf16[128,3584]{1,0:T(8,128)(2,1)} reshape(bf16[64,2,3584]{2,1,0:T(2,128)(2,1)} %all_to_all.16) | data formatting | bytes 1835008 | tf_op jit(solution)/shard_map/reshape | solution.py:13
  189.7 0.0 copy-done.2
  189.7 1.7 fusion.5
  191.4 1.4 convolution_add_fusion
  192.8 6.4 %collective-permute-start.3 = (f32[128,128]{0,1:T(8,128)S(1)}, f32[128,128]{0,1:T(8,128)S(1)}, u32[]{:S(2)}, u32[]{:S(2)}) collective-permute-start(f32[128,128]{0,1:T(8,128)S(1)} %slice_select_fusion), channel_id=1, source_target_pairs={{0,64},{64,0},{128,192},{192,128},{256,320},{320,256},{384,448},{4... | collective-permute-start | bytes 196616 | tf_op jit(solution)/shard_map/ppermute | solution.py:31
  199.3 0.9 collective-permute-done.3
  200.2 0.6 fusion.16
  200.8 1.4 fusion
  (5 shorter events, 0.1 us)
Async XLA Ops:
  0.6 48.1 %copy-start = (bf16[1,3584,128]{2,1,0:T(8,128)(2,1)S(1)}, bf16[1,3584,128]{2,1,0:T(8,128)(2,1)}, u32[]{:S(2)}) copy-start(bf16[1,3584,128]{2,1,0:T(8,128)(2,1)} %param.8) | copy-start | bytes 2752516
  45.7 3.0 %copy-start.3 = (f32[1,128]{1,0:T(1,128)S(1)}, f32[1,128]{1,0:T(1,128)}, u32[]{:S(2)}) copy-start(f32[1,128]{1,0:T(1,128)} %param.9) | copy-start | bytes 1540
  48.7 12.7 %copy-start.1 = (bf16[1,2,2,128,1792]{4,3,2,1,0:T(8,128)(2,1)S(1)}, bf16[1,2,2,128,1792]{4,3,2,1,0:T(8,128)(2,1)}, u32[]{:S(2)}) copy-start(bf16[1,2,2,128,1792]{4,3,2,1,0:T(8,128)(2,1)} %param.10) | copy-start | bytes 5505028
  49.2 13.2 %collective-permute-start = (bf16[128,128]{0,1:T(8,128)(2,1)S(1)}, bf16[128,128]{0,1:T(8,128)(2,1)S(1)}, u32[]{:S(2)}, u32[]{:S(2)}) collective-permute-start(bf16[128,128]{0,1:T(8,128)(2,1)S(1)} %fusion.2), channel_id=1, source_target_pairs={{0,64},{64,0},{128,192},{192,128},{256,320},{320,256},{384,448},{4... | collective-permute-start | bytes 98312 | tf_op jit(solution)/shard_map/ppermute | solution.py:31
  93.6 27.6 %all-to-all-start.1 = ((f32[16,2,3584]{2,1,0:T(2,128)}), f32[16,2,3584]{2,1,0:T(2,128)S(1)}, u32[]{:S(2)}, u32[]{:S(2)}) async-start(f32[16,2,3584]{2,1,0:T(2,128)} %reshape.43), calls=%async_computation.1 | async-start | bytes 917504 | tf_op jit(solution)/shard_map/all_to_all | solution.py:42
  121.4 5.3 %collective-permute-start.1 = (f32[2,1792]{1,0:T(2,128)S(1)}, f32[2,1792]{1,0:T(2,128)S(1)}, u32[]{:S(2)}, u32[]{:S(2)}) collective-permute-start(f32[2,1792]{1,0:T(2,128)S(1)} %get-tuple-element.12), channel_id=1, source_target_pairs={{0,128},{64,192},{128,256},{192,320},{256,384},{320,448},{1,129},{... | collective-permute-start | bytes 43016 | tf_op jit(solution)/shard_map/ppermute | solution.py:54
  124.6 4.5 %collective-permute-start.2 = (f32[2,1792]{1,0:T(2,128)S(1)}, f32[2,1792]{1,0:T(2,128)S(1)}, u32[]{:S(2)}, u32[]{:S(2)}) collective-permute-start(f32[2,1792]{1,0:T(2,128)S(1)} %get-tuple-element.11), channel_id=1, source_target_pairs={{128,0},{192,64},{256,128},{320,192},{384,256},{448,320},{129,1},{... | collective-permute-start | bytes 43016 | tf_op jit(solution)/shard_map/ppermute | solution.py:54
  129.1 60.6 %copy-start.2 = (bf16[2,1792]{1,0:T(2,128)(2,1)}, bf16[2,1792]{1,0:T(2,128)(2,1)S(1)}, u32[]{:S(2)}) copy-start(bf16[2,1792]{1,0:T(2,128)(2,1)S(1)} %get-tuple-element.10) | copy-start | bytes 21508
  192.8 7.3 %collective-permute-start.3 = (f32[128,128]{0,1:T(8,128)S(1)}, f32[128,128]{0,1:T(8,128)S(1)}, u32[]{:S(2)}, u32[]{:S(2)}) collective-permute-start(f32[128,128]{0,1:T(8,128)S(1)} %slice_select_fusion), channel_id=1, source_target_pairs={{0,64},{64,0},{128,192},{192,128},{256,320},{320,256},{384,448},{4... | collective-permute-start | bytes 196616 | tf_op jit(solution)/shard_map/ppermute | solution.py:31
where the time goes:
time: 203 us; the launch traced here: 202 us
  blocking collectives  128 us (63%)
  starting transfers between devices  29.8 us (15%)
  waiting for transfers between devices  24.1 us (12%)
  local copies, waits for them, and re-layouts  7.57 us (4%)
  matrix products  6.75 us (3%)
  other arithmetic  4.76 us (2%)
    all_to_all x1, blocking collectives, sent_to_all(): lax.all_to_all(jnp.broadcast_to(shard[None], (count, *shard.shape)), axis...  56.9 us
    all_gather x2, blocking collectives, all_blocks(): pieces = lax.all_gather(pieces, axes[k], axis=0, tiled=True)  44.3 us
    all_to_all x1, blocking collectives, sent_and_summed(): pieces = lax.all_to_all(split_up(shard, dim, count), axis, 0, 0, tiled=True)  26.5 us
    all_to_all x1, waiting for transfers between devices, sent_and_summed(): pieces = lax.all_to_all(split_up(shard, dim, count), axis, 0, 0, tiled=True)  20.8 us
    ppermute x2, starting transfers between devices, swapped(): lax.ppermute(shard, axis, [(i, i ^ 1 << stride) for i in range(lax.axis_s...  18.6 us
    all_to_all x1, starting transfers between devices, sent_and_summed(): pieces = lax.all_to_all(split_up(shard, dim, count), axis, 0, 0, tiled=True)  6.74 us
    ppermute x2, starting transfers between devices, from_behind(): return lax.ppermute(block, axis, route)  4.47 us
  transfers between devices with their start and end apart: 5, of which 3 were waited for; matrix products, arithmetic and copies ran while one was open for 1% of the time, Pallas kernels for 0%

commit v1 on v0

--- a/solution.py
+++ b/solution.py
@@ -16,7 +16,11 @@
 def all_blocks(shard, axes, sequence):
     pieces = shard[None]
     for k in sequence:
-        pieces = lax.all_gather(pieces, axes[k], axis=0, tiled=True)
+        panel = axes[k]
+        long_array = lax.psum(1, panel)
+        reached = jnp.stack([pieces] * long_array)
+        tmp = lax.all_to_all(reached, panel, 0, 0)
+        pieces = jnp.concatenate(tmp, axis=0)
     held = [lax.axis_size(axes[k]) for k in reversed(sequence)]
     pieces = pieces.reshape(*held, *shard.shape)
     turned = sorted(range(len(sequence)), key=lambda place: sequence[len(sequence) - 1 - place])

time: 203 us -> 218 us (1.074)
  waiting for transfers between devices: 24.1 us -> 62.4 us
  blocking collectives: 128 us -> 92.3 us
  starting transfers between devices: 29.8 us -> 40.6 us
    all_gather x2 -> x0, blocking collectives: 44.3 us -> none  [all_blocks(): pieces = lax.all_gather(pieces, axes[k], axis=0, tiled=True)]
    all_to_all x0 -> x1, waiting for transfers between devices: none -> 38.2 us  [all_blocks(): tmp = lax.all_to_all(reached, panel, 0, 0)]
    all_to_all x0 -> x1, starting transfers between devices: none -> 14.9 us  [all_blocks(): tmp = lax.all_to_all(reached, panel, 0, 0)]
    all_to_all x0 -> x1, blocking collectives: none -> 9.06 us  [all_blocks(): tmp = lax.all_to_all(reached, panel, 0, 0)]
    ppermute x2, starting transfers between devices: 18.6 us -> 12.8 us  [swapped(): lax.ppermute(shard, axis, [(i, i ^ 1 << stride) for i in range(lax.axis_s...]
  transfers between devices with their start and end apart: 5 -> 6, of which waited for: 3 -> 4; matrix products, arithmetic and copies ran while one was open for 1% -> 1% of each run, Pallas kernels for 0% -> 0%
where the time goes in v1:
time: 218 us; the launch traced here: 217 us
  blocking collectives  92.3 us (42%)
  waiting for transfers between devices  62.4 us (29%)
  starting transfers between devices  40.6 us (19%)
  local copies, waits for them, and re-layouts  8.98 us (4%)
  matrix products  6.75 us (3%)
  other arithmetic  4.76 us (2%)
    all_to_all x1, blocking collectives, sent_to_all(): lax.all_to_all(jnp.broadcast_to(shard[None], (count, *shard.shape)), axis...  56.8 us
    all_to_all x1, waiting for transfers between devices, all_blocks(): tmp = lax.all_to_all(reached, panel, 0, 0)  38.2 us
    all_to_all x1, blocking collectives, sent_and_summed(): pieces = lax.all_to_all(split_up(shard, dim, count), axis, 0, 0, tiled=True)  26.5 us
    all_to_all x1, waiting for transfers between devices, sent_and_summed(): pieces = lax.all_to_all(split_up(shard, dim, count), axis, 0, 0, tiled=True)  20.9 us
    all_to_all x1, starting transfers between devices, all_blocks(): tmp = lax.all_to_all(reached, panel, 0, 0)  14.9 us
    ppermute x2, starting transfers between devices, swapped(): lax.ppermute(shard, axis, [(i, i ^ 1 << stride) for i in range(lax.axis_s...  12.8 us
    all_to_all x1, blocking collectives, all_blocks(): tmp = lax.all_to_all(reached, panel, 0, 0)  9.06 us
    all_to_all x1, starting transfers between devices, sent_and_summed(): pieces = lax.all_to_all(split_up(shard, dim, count), axis, 0, 0, tiled=True)  8.35 us
  transfers between devices with their start and end apart: 6, of which 4 were waited for; matrix products, arithmetic and copies ran while one was open for 1% of the time, Pallas kernels for 0%

profile of v1, /device:TPU:1, one launch (start us, length us, event | category | flops | bytes accessed | tf_op | source)
XLA Modules:
  0.0 217.3 jit_solution(11187432214534088455)
XLA Ops:
  0.6 0.0 copy-start
  0.7 0.8 dynamic-slice_bitcast_fusion
  1.5 9.1 %all_to_all.25 = bf16[4,1,2,3584]{3,2,1,0:T(2,128)(2,1)S(1)} all-to-all(bf16[4,1,2,3584]{3,2,1,0:T(2,128)(2,1)S(1)} %stack.6), channel_id=1, replica_groups=mesh['layer'=8,'latent_0'=4,'latent_1'=16] {'latent_0'}, dimensions={0} | all-to-all | bytes 114688 | tf_op jit(solution)/shard_map/all_to_all | solution.py:22
  10.6 1.4 stack.7
  12.0 14.9 %all-to-all-start.1 = ((bf16[16,4,2,3584]{3,2,1,0:T(2,128)(2,1)}), bf16[16,4,2,3584]{3,2,1,0:T(2,128)(2,1)S(1)}, u32[]{:S(2)}, u32[]{:S(2)}) async-start(bf16[16,4,2,3584]{3,2,1,0:T(2,128)(2,1)} %stack.7), calls=%async_computation.1 | async-start | bytes 1835008 | tf_op jit(solution)/shard_map/all_to_all | solution.py:22
  26.9 1.3 compare_reduce_fusion
  28.9 38.2 %all-to-all-done.1 = bf16[16,4,2,3584]{3,2,1,0:T(2,128)(2,1)S(1)} async-done(((bf16[16,4,2,3584]{3,2,1,0:T(2,128)(2,1)}), bf16[16,4,2,3584]{3,2,1,0:T(2,128)(2,1)S(1)}, u32[]{:S(2)}, u32[]{:S(2)}) %all-to-all-start.1) | async-done | bytes 917536 | tf_op jit(solution)/shard_map/all_to_all | solution.py:22
  67.1 0.0 copy-start.3
  67.1 0.6 copy.19
  67.7 0.3 reshape_reshape.3
  68.1 0.0 copy-start.1
  68.1 0.0 copy-done
  68.1 0.0 copy-done.3
  68.1 0.4 fusion.2
  68.6 6.4 %collective-permute-start = (bf16[128,128]{0,1:T(8,128)(2,1)S(1)}, bf16[128,128]{0,1:T(8,128)(2,1)S(1)}, u32[]{:S(2)}, u32[]{:S(2)}) collective-permute-start(bf16[128,128]{0,1:T(8,128)(2,1)S(1)} %fusion.2), channel_id=1, source_target_pairs={{0,64},{64,0},{128,192},{192,128},{256,320},{320,256},{384,448},{4... | collective-permute-start | bytes 98312 | tf_op jit(solution)/shard_map/ppermute | solution.py:35
  75.0 0.0 copy-done.1
  75.0 1.0 fusion.17
  76.0 0.0 collective-permute-done
  76.1 1.5 fusion.8
  77.6 0.3 fusion.7
  77.9 0.2 pad_maximum_fusion
  78.1 26.5 %all_to_all.26 = f32[4,32,3584]{2,1,0:T(8,128)} all-to-all(f32[4,32,3584]{2,1,0:T(8,128)S(1)} %bitcast.38), channel_id=1, replica_groups=mesh['layer'=8,'latent_0'=4,'latent_1'=16] {'latent_0'}, dimensions={0} | all-to-all | bytes 3670016 | tf_op jit(solution)/shard_map/all_to_all | solution.py:46
  104.5 1.6 reduce_sum.27
  106.2 1.0 reshape.45
  107.2 8.4 %all-to-all-start.3 = ((f32[16,2,3584]{2,1,0:T(2,128)}), f32[16,2,3584]{2,1,0:T(2,128)S(1)}, u32[]{:S(2)}, u32[]{:S(2)}) async-start(f32[16,2,3584]{2,1,0:T(2,128)} %reshape.45), calls=%async_computation.3 | async-start | bytes 917504 | tf_op jit(solution)/shard_map/all_to_all | solution.py:46
  115.6 20.9 %all-to-all-done.3 = f32[16,2,3584]{2,1,0:T(2,128)S(1)} async-done(((f32[16,2,3584]{2,1,0:T(2,128)}), f32[16,2,3584]{2,1,0:T(2,128)S(1)}, u32[]{:S(2)}, u32[]{:S(2)}) %all-to-all-start.3) | async-done | bytes 458784 | tf_op jit(solution)/shard_map/all_to_all | solution.py:46
  136.5 0.1 reduce_sum.28
  136.6 3.2 %collective-permute-start.1 = (f32[2,1792]{1,0:T(2,128)S(1)}, f32[2,1792]{1,0:T(2,128)S(1)}, u32[]{:S(2)}, u32[]{:S(2)}) collective-permute-start(f32[2,1792]{1,0:T(2,128)S(1)} %get-tuple-element.12), channel_id=1, source_target_pairs={{0,128},{64,192},{128,256},{192,320},{256,384},{320,448},{1,129},{... | collective-permute-start | bytes 43016 | tf_op jit(solution)/shard_map/ppermute | solution.py:58
  139.8 1.3 collective-permute-start.2
  141.1 0.8 dynamic-slice_convert_fusion
  141.9 0.0 collective-permute-done.1
  142.0 2.3 %collective-permute-done.2 = f32[2,1792]{1,0:T(2,128)S(1)} collective-permute-done((f32[2,1792]{1,0:T(2,128)S(1)}, f32[2,1792]{1,0:T(2,128)S(1)}, u32[]{:S(2)}, u32[]{:S(2)}) %collective-permute-start.2) | collective-permute-done | bytes 14368 | tf_op jit(solution)/shard_map/ppermute | solution.py:58
  144.3 0.0 copy-start.2
  144.4 0.5 broadcast_in_dim.17
  144.8 56.8 %all_to_all.27 = bf16[64,2,3584]{2,1,0:T(2,128)(2,1)} all-to-all(bf16[64,2,3584]{2,1,0:T(2,128)(2,1)S(1)} %broadcast_in_dim.17), channel_id=1, replica_groups=mesh['layer'=8,'latent_0'=4,'latent_1'=16] {'latent_0','latent_1'}, dimensions={0} | all-to-all | bytes 1835008 | tf_op jit(solution)/shard_map/all_to_all | solution.py:63
  201.6 3.2 %reshape.46 = bf16[128,3584]{1,0:T(8,128)(2,1)} reshape(bf16[64,2,3584]{2,1,0:T(2,128)(2,1)} %all_to_all.27) | data formatting | bytes 1835008 | tf_op jit(solution)/shard_map/reshape | solution.py:13
  204.8 0.0 copy-done.2
  204.8 1.7 fusion.5
  206.5 1.4 convolution_add_fusion
  208.0 6.4 %collective-permute-start.3 = (f32[128,128]{0,1:T(8,128)S(1)}, f32[128,128]{0,1:T(8,128)S(1)}, u32[]{:S(2)}, u32[]{:S(2)}) collective-permute-start(f32[128,128]{0,1:T(8,128)S(1)} %slice_select_fusion), channel_id=1, source_target_pairs={{0,64},{64,0},{128,192},{192,128},{256,320},{320,256},{384,448},{4... | collective-permute-start | bytes 196616 | tf_op jit(solution)/shard_map/ppermute | solution.py:35
  214.4 0.9 collective-permute-done.3
  215.3 0.6 fusion.16
  215.9 1.4 fusion
  (6 shorter events, 0.1 us)
Async XLA Ops:
  0.6 67.5 %copy-start = (bf16[1,3584,128]{2,1,0:T(8,128)(2,1)S(1)}, bf16[1,3584,128]{2,1,0:T(8,128)(2,1)}, u32[]{:S(2)}) copy-start(bf16[1,3584,128]{2,1,0:T(8,128)(2,1)} %param.8) | copy-start | bytes 2752516
  12.0 55.1 %all-to-all-start.1 = ((bf16[16,4,2,3584]{3,2,1,0:T(2,128)(2,1)}), bf16[16,4,2,3584]{3,2,1,0:T(2,128)(2,1)S(1)}, u32[]{:S(2)}, u32[]{:S(2)}) async-start(bf16[16,4,2,3584]{3,2,1,0:T(2,128)(2,1)} %stack.7), calls=%async_computation.1 | async-start | bytes 1835008 | tf_op jit(solution)/shard_map/all_to_all | solution.py:22
  67.1 1.0 copy-start.3
  68.1 6.9 %copy-start.1 = (bf16[1,2,2,128,1792]{4,3,2,1,0:T(8,128)(2,1)S(1)}, bf16[1,2,2,128,1792]{4,3,2,1,0:T(8,128)(2,1)}, u32[]{:S(2)}) copy-start(bf16[1,2,2,128,1792]{4,3,2,1,0:T(8,128)(2,1)} %param.10) | copy-start | bytes 5505028
  68.6 7.5 %collective-permute-start = (bf16[128,128]{0,1:T(8,128)(2,1)S(1)}, bf16[128,128]{0,1:T(8,128)(2,1)S(1)}, u32[]{:S(2)}, u32[]{:S(2)}) collective-permute-start(bf16[128,128]{0,1:T(8,128)(2,1)S(1)} %fusion.2), channel_id=1, source_target_pairs={{0,64},{64,0},{128,192},{192,128},{256,320},{320,256},{384,448},{4... | collective-permute-start | bytes 98312 | tf_op jit(solution)/shard_map/ppermute | solution.py:35
  107.2 29.3 %all-to-all-start.3 = ((f32[16,2,3584]{2,1,0:T(2,128)}), f32[16,2,3584]{2,1,0:T(2,128)S(1)}, u32[]{:S(2)}, u32[]{:S(2)}) async-start(f32[16,2,3584]{2,1,0:T(2,128)} %reshape.45), calls=%async_computation.3 | async-start | bytes 917504 | tf_op jit(solution)/shard_map/all_to_all | solution.py:46
  136.6 5.3 %collective-permute-start.1 = (f32[2,1792]{1,0:T(2,128)S(1)}, f32[2,1792]{1,0:T(2,128)S(1)}, u32[]{:S(2)}, u32[]{:S(2)}) collective-permute-start(f32[2,1792]{1,0:T(2,128)S(1)} %get-tuple-element.12), channel_id=1, source_target_pairs={{0,128},{64,192},{128,256},{192,320},{256,384},{320,448},{1,129},{... | collective-permute-start | bytes 43016 | tf_op jit(solution)/shard_map/ppermute | solution.py:58
  139.8 4.5 %collective-permute-start.2 = (f32[2,1792]{1,0:T(2,128)S(1)}, f32[2,1792]{1,0:T(2,128)S(1)}, u32[]{:S(2)}, u32[]{:S(2)}) collective-permute-start(f32[2,1792]{1,0:T(2,128)S(1)} %get-tuple-element.11), channel_id=1, source_target_pairs={{128,0},{192,64},{256,128},{320,192},{384,256},{448,320},{129,1},{... | collective-permute-start | bytes 43016 | tf_op jit(solution)/shard_map/ppermute | solution.py:58
  144.3 60.5 %copy-start.2 = (bf16[2,1792]{1,0:T(2,128)(2,1)}, bf16[2,1792]{1,0:T(2,128)(2,1)S(1)}, u32[]{:S(2)}) copy-start(bf16[2,1792]{1,0:T(2,128)(2,1)S(1)} %get-tuple-element.10) | copy-start | bytes 21508
  208.0 7.3 %collective-permute-start.3 = (f32[128,128]{0,1:T(8,128)S(1)}, f32[128,128]{0,1:T(8,128)S(1)}, u32[]{:S(2)}, u32[]{:S(2)}) collective-permute-start(f32[128,128]{0,1:T(8,128)S(1)} %slice_select_fusion), channel_id=1, source_target_pairs={{0,64},{64,0},{128,192},{192,128},{256,320},{320,256},{384,448},{4... | collective-permute-start | bytes 196616 | tf_op jit(solution)/shard_map/ppermute | solution.py:35
